TPU v7x, 256 devices: a whole 4x4x8 slice. The times are simulated.
256 devices in a mesh: tm: 8 (over z), height: 16 (over x, y), width: 2 (over core).
Axes of the slice: x: 4, y: 4, z: 8, core: 2. Of those that a mesh axis runs over, the one named last changes fastest.
Arguments:
- video: bfloat16 [2, 128, 16, 256, 128], P('width', ('tm', 'height')), may hold values from -6 to 6
- out_grad: bfloat16 [2, 128, 16, 256, 128], P('width', None, 'tm', 'height'), may hold values from -6 to 6
- lengths: int32 [4], replicated, may hold values from 1 to 6, 16 in all
- temporal_weight: bfloat16 [3, 128, 128], replicated, may hold values from -0.3125 to 0.3125
- spatial_weight: bfloat16 [3, 3, 128, 128], replicated, may hold values from -0.1875 to 0.1875
Outputs:
- video_grad: bfloat16 [2, 128, 16, 256, 128], P('width', ('tm', 'height'))
- temporal_grad: float32 [3, 128, 128], replicated
- spatial_grad: float32 [3, 3, 128, 128], replicated
Inputs may be any that keep to these rules, and one draw needn't show every extreme that they name: The 4 clips lie end to end in frame order, their lengths sum to 16, and the longest clip has exactly 6 frames.
All inputs are finite; a program needn't handle non-finite values.
Results may differ from a plain program's by a relative error of at most 0.008.
Values may be sent and summed in bfloat16 or wider, within the bound.
A program may use at most 128 MiB of HBM per device.

v0:
```python
import jax
import jax.numpy as jnp
from jax import lax
from jax.sharding import PartitionSpec as P


def with_halo(cells, sides, width):
    for axis, dim in sides:
        count = lax.axis_size(axis)
        ends = count - 1
        head = lax.slice_in_dim(cells, 0, width, axis=dim)
        tail = lax.slice_in_dim(cells, cells.shape[dim] - width, cells.shape[dim], axis=dim)
        cells = jnp.concatenate(
            [
                lax.ppermute(tail, axis, [(i, (i + 1) % count) for i in range(ends)]),
                cells,
                lax.ppermute(head, axis, [((i + 1) % count, i) for i in range(ends)]),
            ],
            axis=dim,
        )
    return cells


def frame_masks(lengths, frames):
    ends = jnp.cumsum(lengths, dtype=jnp.int32)
    starts = ends - lengths
    frame_index = jnp.arange(frames, dtype=jnp.int32)
    inside = (frame_index[:, None] >= starts[None, :]) & (frame_index[:, None] < ends[None, :])
    first = jnp.sum(jnp.where(inside, starts[None, :], 0), axis=1, dtype=jnp.int32)
    return jnp.stack([frame_index - lag >= first for lag in range(3)]).astype(jnp.bfloat16)


def silu_slope(pre, grads):
    sig = jax.nn.sigmoid(pre)
    return grads.astype(jnp.float32) * sig * (1.0 + pre * (1.0 - sig))


def flatten(block):
    return block.reshape(-1, block.shape[-1])


def spatial_forward(padded, weights, cols, rows):
    total = None
    for row_off in range(3):
        for col_off in range(3):
            piece = flatten(padded[col_off : col_off + cols, :, row_off : row_off + rows])
            term = jnp.dot(piece, weights[row_off, col_off], preferred_element_type=jnp.float32)
            total = term if total is None else total + term
    return total


def shards(video, out_grad, lengths, temporal_weight, spatial_weight):
    width_loc = video.shape[1]
    frames = video.shape[2]
    rows = video.shape[3]
    chans = video.shape[4]
    n_tm = lax.axis_size("tm")
    n_height = lax.axis_size("height")
    frames_dev = frames // n_tm
    rows_dev = rows // n_height
    cols_half = out_grad.shape[1]
    total_cols = cols_half * lax.axis_size("width")
    masks = frame_masks(lengths, frames)
    local_video = video[0]
    padded_video = jnp.pad(local_video, ((0, 0), (2, 0), (0, 0), (0, 0)))
    taps = [
        padded_video[:, 2 - lag : 2 - lag + frames] * masks[lag][None, :, None, None]
        for lag in range(3)
    ]
    total = None
    for lag in range(3):
        term = jnp.dot(flatten(taps[lag]), temporal_weight[lag], preferred_element_type=jnp.float32)
        total = term if total is None else total + term
    act_time = total.astype(jnp.bfloat16).reshape(local_video.shape)
    arranged = act_time.reshape(width_loc, n_tm, frames_dev, n_height, rows_dev, chans)
    arranged = arranged.transpose(1, 3, 0, 2, 4, 5).reshape(
        n_tm * n_height * width_loc, frames_dev, rows_dev, chans
    )
    act_space = lax.all_to_all(arranged, ("tm", "height"), split_axis=0, concat_axis=0, tiled=True)
    grad_space = out_grad[0]
    padded_act = with_halo(act_space, (("height", 2), ("width", 0)), 1)
    pre = spatial_forward(padded_act, spatial_weight, cols_half, rows_dev)
    delta = silu_slope(pre, flatten(grad_space)).astype(jnp.bfloat16).reshape(act_space.shape)
    padded_delta = with_halo(delta, (("height", 2), ("width", 0)), 1)
    flat_delta = flatten(delta)
    back = None
    spatial_terms = []
    for row_off in range(3):
        line = []
        for col_off in range(3):
            piece = flatten(
                padded_delta[
                    2 - col_off : 2 - col_off + cols_half, :, 2 - row_off : 2 - row_off + rows_dev
                ]
            )
            term = jnp.dot(
                piece, spatial_weight[row_off, col_off].T, preferred_element_type=jnp.float32
            )
            back = term if back is None else back + term
            source = flatten(
                padded_act[col_off : col_off + cols_half, :, row_off : row_off + rows_dev]
            )
            line.append(
                lax.dot_general(
                    source, flat_delta, (((0,), (0,)), ((), ())), preferred_element_type=jnp.float32
                )
            )
        spatial_terms.append(jnp.stack(line))
    spatial_local = jnp.stack(spatial_terms)
    grad_act_space = back.astype(jnp.bfloat16).reshape(act_space.shape)
    received = lax.all_to_all(
        grad_act_space, ("tm", "height"), split_axis=0, concat_axis=0, tiled=True
    )
    received = received.reshape(n_tm, n_height, width_loc, frames_dev, rows_dev, chans)
    grad_time = received.transpose(2, 0, 3, 1, 4, 5).reshape(width_loc, frames, rows, chans)
    flat_grad = flatten(grad_time)
    frame_total = None
    temporal_terms = []
    for lag in range(3):
        temporal_terms.append(
            lax.dot_general(
                flatten(taps[lag]),
                flat_grad,
                (((0,), (0,)), ((), ())),
                preferred_element_type=jnp.float32,
            )
        )
        masked = flatten(grad_time * masks[lag][None, :, None, None])
        product = jnp.dot(
            masked, temporal_weight[lag].T, preferred_element_type=jnp.float32
        ).reshape(grad_time.shape)
        moved = jnp.pad(product[:, lag:], ((0, 0), (0, lag), (0, 0), (0, 0)))
        frame_total = moved if frame_total is None else frame_total + moved
    temporal_local = jnp.stack(temporal_terms)
    video_grad = frame_total.astype(jnp.bfloat16)[None]
    scale = float(frames * rows * total_cols) ** (-0.5)
    temporal_grad, spatial_grad = lax.psum(
        (temporal_local * scale, spatial_local * scale), ("tm", "height", "width")
    )
    return (video_grad, temporal_grad, spatial_grad)


def solution(mesh):
    placed = (
        P("width", ("tm", "height"), None, None, None),
        P("width", None, "tm", "height", None),
        P(),
        P(),
        P(),
    )
    return jax.shard_map(
        shards,
        mesh=mesh,
        in_specs=placed,
        out_specs=(P("width", ("tm", "height"), None, None, None), P(), P()),
        check_vma=False,
    )
```

profile of v0, /device:TPU:2, one launch (start us, length us, event | category | flops | bytes accessed | tf_op | source)
XLA Modules:
  0.0 414.0 jit_solution(14738831127467204281)
XLA Ops:
  7.2 0.9 reduce-window.8
  8.0 0.7 bitcast_subtract_fusion
  8.8 1.4 broadcast_multiply_fusion
  10.6 1.2 copy-done.15
  12.5 0.5 copy-done.11
  13.3 0.4 fusion.2
  14.0 46.1 %all_to_all.10 = bf16[128,2,16,128]{3,2,1,0:T(8,128)(2,1)S(1)} all-to-all(bf16[128,2,16,128]{3,2,1,0:T(8,128)(2,1)S(1)} %bitcast.249), channel_id=1, replica_groups=mesh['tm'=8,'height'=16,'width'=2] {'tm','height'}, dimensions={0} | all-to-all | bytes 2097152 | tf_op jit(solution)/shard_map/all_to_all | solution.py:79
  60.2 2.4 collective-permute-start
  62.7 5.5 %collective-permute-start.1 = (bf16[128,2,1,128]{3,2,1,0:T(2,128)(2,1)S(1)}, bf16[128,2,1,128]{3,2,1,0:T(2,128)(2,1)S(1)}, u32[]{:S(2)}, u32[]{:S(2)}) collective-permute-start(bf16[128,2,1,128]{3,2,1,0:T(2,128)(2,1)S(1)} %get-tuple-element.38), channel_id=1, source_target_pairs={{2,0},{4,2},{6,4},{8,6},{10,8},{12,10},{14,12},{16,14},{18,16},{20... | collective-permute-start | bytes 196616 | tf_op jit(solution)/shard_map/ppermute | solution.py:17
  68.5 0.7 collective-permute-done
  69.2 1.5 collective-permute-done.1
  70.7 1.3 collective-permute-start.2
  72.0 1.3 collective-permute-start.3
  73.3 1.0 pad_maximum_fusion.4
  75.1 2.0 maximum_maximum_fusion
  77.1 1.3 fusion.67
  78.9 0.4 convolution_add_fusion.13
  81.5 0.4 convolution_add_fusion.9
  82.0 0.4 convolution_add_fusion.8
  82.4 0.8 copy-done.20
  83.2 1.1 fusion.5
  84.4 1.9 collective-permute-start.4
  86.4 6.6 %collective-permute-start.5 = (bf16[128,2,1,128]{3,2,1,0:T(2,128)(2,1)S(1)}, bf16[128,2,1,128]{3,2,1,0:T(2,128)(2,1)S(1)}, u32[]{:S(2)}, u32[]{:S(2)}) collective-permute-start(bf16[128,2,1,128]{3,2,1,0:T(2,128)(2,1)S(1)} %get-tuple-element.34), channel_id=1, source_target_pairs={{2,0},{4,2},{6,4},{8,6},{10,8},{12,10},{14,12},{16,14},{18,16},{20... | collective-permute-start | bytes 196616 | tf_op jit(solution)/shard_map/ppermute | solution.py:17
  93.0 0.5 convolution_bitcast_fusion.9
  93.5 1.6 collective-permute-done.4
  95.1 1.5 collective-permute-done.5
  96.6 1.3 collective-permute-start.6
  97.9 3.0 collective-permute-start.7
  101.0 1.0 pad_maximum_fusion.2
  102.0 0.4 fusion.30
  102.4 2.0 pad_maximum_fusion.1
  104.4 0.6 fusion.65
  105.1 0.6 fusion.66
  105.7 0.4 convolution_add_fusion.6
  106.2 0.4 convolution_add_fusion.5
  106.6 0.4 convolution_add_fusion.4
  107.0 0.4 convolution_add_fusion.3
  107.5 0.4 fusion.14
  107.9 0.4 convolution_add_fusion.2
  108.3 0.4 convolution_add_fusion.1
  108.8 1.4 fusion.3
  110.2 10.4 %all-to-all-start.1 = ((bf16[128,2,16,128]{3,2,1,0:T(8,128)(2,1)}), bf16[128,2,16,128]{3,2,1,0:T(8,128)(2,1)}, u32[]{:S(2)}, u32[]{:S(2)}) async-start(bf16[128,2,16,128]{3,2,1,0:T(8,128)(2,1)} %bitcast.251), calls=%async_computation.1 | async-start | bytes 2097152 | tf_op jit(solution)/shard_map/all_to_all | solution.py:111
  120.9 1.8 convolution_bitcast_fusion.10
  122.8 0.5 convolution_bitcast_fusion.8
  123.3 0.5 convolution_bitcast_fusion.5
  124.0 0.5 convolution_bitcast_fusion.7
  124.5 0.5 convolution_bitcast_fusion.6
  125.2 0.5 convolution_bitcast_fusion.3
  125.8 0.5 convolution_bitcast_fusion.2
  126.3 0.5 convolution_bitcast_fusion.4
  126.8 0.9 maximum_multiply_fusion
  127.7 23.3 %all-to-all-done.1 = bf16[128,2,16,128]{3,2,1,0:T(8,128)(2,1)} async-done(((bf16[128,2,16,128]{3,2,1,0:T(8,128)(2,1)}), bf16[128,2,16,128]{3,2,1,0:T(8,128)(2,1)}, u32[]{:S(2)}, u32[]{:S(2)}) %all-to-all-start.1) | async-done | bytes 1048608 | tf_op jit(solution)/shard_map/all_to_all | solution.py:111
  150.9 1.5 copy.12
  152.5 0.5 convolution_bitcast_fusion.11
  153.0 0.5 convolution_bitcast_fusion.12
  153.7 0.5 convolution_bitcast_fusion.13
  154.2 0.7 maximum_multiply_fusion.1
  154.9 1.5 bitcast_multiply_fusion.2
  156.4 0.4 convolution_bitcast_fusion.1
  157.1 0.4 convolution_bitcast_fusion
  157.6 1.4 fusion.8
  159.1 244.5 %all-reduce.6.cloned.1.call-done = (f32[3,128,128]{2,1,0:T(8,128)}, f32[3,3,128,128]{3,2,1,0:T(8,128)}) async-done(((f32[3,128,128]{2,1,0:T(8,128)}, f32[3,3,128,128]{3,2,1,0:T(8,128)}), (f32[3,128,128]{2,1,0:T(8,128)}, f32[3,3,128,128]{3,2,1,0:T(8,128)})) %all-reduce.6.cloned.1.call-update) | async-done | bytes 786448 | tf_op jit(solution)/shard_map/psum | solution.py:137
  403.6 1.6 copy.18
  405.2 1.9 copy.19
  (70 shorter events, 7.1 us)
Async XLA Ops:
  7.2 3.1 copy-start.19
  10.2 1.8 copy-start.9
  10.2 1.6 copy-start.15
  12.0 1.0 copy-start.11
  12.0 1.3 copy-start.13
  60.2 9.0 %collective-permute-start = (bf16[128,2,1,128]{3,2,1,0:T(2,128)(2,1)S(1)}, bf16[128,2,1,128]{3,2,1,0:T(2,128)(2,1)S(1)}, u32[]{:S(2)}, u32[]{:S(2)}) collective-permute-start(bf16[128,2,1,128]{3,2,1,0:T(2,128)(2,1)S(1)} %get-tuple-element.37), channel_id=1, source_target_pairs={{0,2},{2,4},{4,6},{6,8},{8,10},{10,12},{12,14},{14,16},{16,18},{18... | collective-permute-start | bytes 196616 | tf_op jit(solution)/shard_map/ppermute | solution.py:15
  62.7 8.0 %collective-permute-start.1 = (bf16[128,2,1,128]{3,2,1,0:T(2,128)(2,1)S(1)}, bf16[128,2,1,128]{3,2,1,0:T(2,128)(2,1)S(1)}, u32[]{:S(2)}, u32[]{:S(2)}) collective-permute-start(bf16[128,2,1,128]{3,2,1,0:T(2,128)(2,1)S(1)} %get-tuple-element.38), channel_id=1, source_target_pairs={{2,0},{4,2},{6,4},{8,6},{10,8},{12,10},{14,12},{16,14},{18,16},{20... | collective-permute-start | bytes 196616 | tf_op jit(solution)/shard_map/ppermute | solution.py:17
  68.5 5.9 %copy-start.18 = (bf16[3,3,128,128]{3,2,1,0:T(8,128)(2,1)S(1)}, bf16[3,3,128,128]{3,2,1,0:T(8,128)(2,1)}, u32[]{:S(2)}) copy-start(bf16[3,3,128,128]{3,2,1,0:T(8,128)(2,1)} %param.9) | copy-start | bytes 884740
  70.7 4.1 collective-permute-start.2
  72.0 3.1 collective-permute-start.3
  74.4 8.0 %copy-start.16 = (bf16[128,2,16,128]{3,2,1,0:T(8,128)(2,1)}, bf16[128,2,16,128]{3,2,1,0:T(8,128)(2,1)S(1)}, u32[]{:S(2)}) copy-start(bf16[128,2,16,128]{3,2,1,0:T(8,128)(2,1)S(1)} %get-tuple-element.35) | copy-start | bytes 3145732
  78.4 1.0 copy-start
  78.5 1.4 copy-start.8
  78.5 1.8 copy-start.6
  78.5 2.2 copy-start.2
  78.5 3.0 copy-start.4
  81.9 1.2 copy-start.20
  84.4 10.6 %collective-permute-start.4 = (bf16[128,2,1,128]{3,2,1,0:T(2,128)(2,1)S(1)}, bf16[128,2,1,128]{3,2,1,0:T(2,128)(2,1)S(1)}, u32[]{:S(2)}, u32[]{:S(2)}) collective-permute-start(bf16[128,2,1,128]{3,2,1,0:T(2,128)(2,1)S(1)} %get-tuple-element.33), channel_id=1, source_target_pairs={{0,2},{2,4},{4,6},{6,8},{8,10},{10,12},{12,14},{14,16},{16,18},{18... | collective-permute-start | bytes 196616 | tf_op jit(solution)/shard_map/ppermute | solution.py:15
  86.4 10.2 %collective-permute-start.5 = (bf16[128,2,1,128]{3,2,1,0:T(2,128)(2,1)S(1)}, bf16[128,2,1,128]{3,2,1,0:T(2,128)(2,1)S(1)}, u32[]{:S(2)}, u32[]{:S(2)}) collective-permute-start(bf16[128,2,1,128]{3,2,1,0:T(2,128)(2,1)S(1)} %get-tuple-element.34), channel_id=1, source_target_pairs={{2,0},{4,2},{6,4},{8,6},{10,8},{12,10},{14,12},{16,14},{18,16},{20... | collective-permute-start | bytes 196616 | tf_op jit(solution)/shard_map/ppermute | solution.py:17
  96.6 5.8 %collective-permute-start.6 = (bf16[1,2,18,128]{3,2,1,0:T(8,128)(2,1)S(1)}, bf16[1,2,18,128]{3,2,1,0:T(8,128)(2,1)S(1)}, u32[]{:S(2)}, u32[]{:S(2)}) collective-permute-start(bf16[1,2,18,128]{3,2,1,0:T(8,128)(2,1)S(1)} %get-tuple-element.22), channel_id=1, source_target_pairs={{1,0},{3,2},{5,4},{7,6},{9,8},{11,10},{13,12},{15,14},{17,16},{19,... | collective-permute-start | bytes 27656 | tf_op jit(solution)/shard_map/ppermute | solution.py:17
  97.9 4.5 %collective-permute-start.7 = (bf16[1,2,18,128]{3,2,1,0:T(8,128)(2,1)S(1)}, bf16[1,2,18,128]{3,2,1,0:T(8,128)(2,1)S(1)}, u32[]{:S(2)}, u32[]{:S(2)}) collective-permute-start(bf16[1,2,18,128]{3,2,1,0:T(8,128)(2,1)S(1)} %get-tuple-element.23), channel_id=1, source_target_pairs={{0,1},{2,3},{4,5},{6,7},{8,9},{10,11},{12,13},{14,15},{16,17},{18,... | collective-permute-start | bytes 27656 | tf_op jit(solution)/shard_map/ppermute | solution.py:15
  110.2 40.7 %all-to-all-start.1 = ((bf16[128,2,16,128]{3,2,1,0:T(8,128)(2,1)}), bf16[128,2,16,128]{3,2,1,0:T(8,128)(2,1)}, u32[]{:S(2)}, u32[]{:S(2)}) async-start(bf16[128,2,16,128]{3,2,1,0:T(8,128)(2,1)} %bitcast.251), calls=%async_computation.1 | async-start | bytes 2097152 | tf_op jit(solution)/shard_map/all_to_all | solution.py:111
  120.6 282.9 %all-reduce.6.cloned.1.call-start = ((), (), s32[]{:S(2)}) async-start(), calls=%async_computation.2 | async-start | bytes 1572864 | tf_op jit(solution)/shard_map/psum | solution.py:137
  120.9 1.9 copy-start.7
  120.9 2.4 copy-start.5
  122.8 1.2 copy-start.3
  124.0 1.2 copy-start.17
  124.5 1.3 copy-start.1
  126.8 25.7 %copy-start.14 = (bf16[1,16,256,128]{3,2,1,0:T(8,128)(2,1)S(1)}, bf16[1,16,256,128]{3,2,1,0:T(8,128)(2,1)}, u32[]{:S(2)}) copy-start(bf16[1,16,256,128]{3,2,1,0:T(8,128)(2,1)} %copy-done.13) | copy-start | bytes 3145732
  150.9 2.0 copy-start.12
  152.5 1.2 copy-start.10
Sparse Core Ops, SparseCore 0:
  155.1 248.4 all-reduce.5
where the time goes:
time: 415 us; the launch traced here: 414 us
  waiting for transfers between devices  273 us (66%)
  blocking collectives  46.1 us (11%)
  starting transfers between devices  34.1 us (8%)
  matrix products  20 us (5%)
  between operations  14.7 us (4%)
  local copies, waits for them, and re-layouts  13.4 us (3%)
  other arithmetic  12.4 us (3%)
    psum x1, waiting for transfers between devices, shards(): lax.psum((temporal_local * scale, spatial_local * scale), ('tm', 'height'...  245 us
    all_to_all x1, blocking collectives, shards(): lax.all_to_all(arranged, ('tm', 'height'), split_axis=0, concat_axis=0, t...  46.1 us
    all_to_all x1, waiting for transfers between devices, shards(): lax.all_to_all(grad_act_space, ('tm', 'height'), split_axis=0, concat_axi...  23.3 us
    ppermute x4, starting transfers between devices, with_halo(): lax.ppermute(head, axis, [((i + 1) % count, i) for i in range(ends)])  14.7 us
    all_to_all x1, starting transfers between devices, shards(): lax.all_to_all(grad_act_space, ('tm', 'height'), split_axis=0, concat_axi...  10.4 us
    ppermute x4, starting transfers between devices, with_halo(): lax.ppermute(tail, axis, [(i, (i + 1) % count) for i in range(ends)])  8.68 us
  transfers between devices with their start and end apart: 10, of which 7 were waited for; matrix products, arithmetic and copies ran while one was open for 3% of the time, Pallas kernels for 0%

commit v1 on v0

--- a/solution.py
+++ b/solution.py
@@ -2,6 +2,7 @@
 import jax.numpy as jnp
 from jax import lax
 from jax.sharding import PartitionSpec as P
+from jax.lax import psum
 
 
 def with_halo(cells, sides, width):
@@ -134,8 +135,8 @@
     temporal_local = jnp.stack(temporal_terms)
     video_grad = frame_total.astype(jnp.bfloat16)[None]
     scale = float(frames * rows * total_cols) ** (-0.5)
-    temporal_grad, spatial_grad = lax.psum(
-        (temporal_local * scale, spatial_local * scale), ("tm", "height", "width")
+    temporal_grad, spatial_grad = psum(
+        psum((temporal_local * scale, spatial_local * scale), ("height", "width")), "tm"
     )
     return (video_grad, temporal_grad, spatial_grad)
 

time: 415 us -> 351 us (0.85)
  waiting for transfers between devices: 273 us -> 209 us
    psum x1 -> x2, waiting for transfers between devices: 245 us -> 180 us  [the longest x1 107 us: shards(): psum((temporal_local * scale, spatial_local * scale), ('height', 'width'))]
  transfers between devices with their start and end apart: 10 -> 11, of which waited for: 7 -> 8; matrix products, arithmetic and copies ran while one was open for 3% -> 4% of each run, Pallas kernels for 0% -> 0%
where the time goes in v1:
time: 351 us; the launch traced here: 350 us
  waiting for transfers between devices  209 us (60%)
  blocking collectives  46.1 us (13%)
  starting transfers between devices  34.2 us (10%)
  matrix products  19.9 us (6%)
  between operations  14.7 us (4%)
  local copies, waits for them, and re-layouts  13.5 us (4%)
  other arithmetic  12.4 us (4%)
    psum x1, waiting for transfers between devices, shards(): psum((temporal_local * scale, spatial_local * scale), ('height', 'width'))  107 us
    psum x1, waiting for transfers between devices, shards(): psum(psum((temporal_local * scale, spatial_local * scale), ('height', 'wi...  73 us
    all_to_all x1, blocking collectives, shards(): lax.all_to_all(arranged, ('tm', 'height'), split_axis=0, concat_axis=0, t...  46.1 us
    all_to_all x1, waiting for transfers between devices, shards(): lax.all_to_all(grad_act_space, ('tm', 'height'), split_axis=0, concat_axi...  23.3 us
    ppermute x4, starting transfers between devices, with_halo(): lax.ppermute(head, axis, [((i + 1) % count, i) for i in range(ends)])  14.9 us
    all_to_all x1, starting transfers between devices, shards(): lax.all_to_all(grad_act_space, ('tm', 'height'), split_axis=0, concat_axi...  10.4 us
    ppermute x4, starting transfers between devices, with_halo(): lax.ppermute(tail, axis, [(i, (i + 1) % count) for i in range(ends)])  8.68 us
    unnamed x44, local copies, waits for them, and re-layouts  8.11 us
  transfers between devices with their start and end apart: 11, of which 8 were waited for; matrix products, arithmetic and copies ran while one was open for 4% of the time, Pallas kernels for 0%

profile of v1, /device:TPU:2, one launch (start us, length us, event | category | flops | bytes accessed | tf_op | source)
XLA Modules:
  0.0 350.2 jit_solution(6964326142621228393)
XLA Ops:
  7.2 0.9 reduce-window.8
  8.0 0.7 bitcast_subtract_fusion
  8.8 1.4 broadcast_multiply_fusion
  10.6 1.2 copy-done.15
  12.5 0.5 copy-done.11
  14.0 46.1 %all_to_all.10 = bf16[128,2,16,128]{3,2,1,0:T(8,128)(2,1)S(1)} all-to-all(bf16[128,2,16,128]{3,2,1,0:T(8,128)(2,1)S(1)} %bitcast.249), channel_id=1, replica_groups=mesh['tm'=8,'height'=16,'width'=2] {'tm','height'}, dimensions={0} | all-to-all | bytes 2097152 | tf_op jit(solution)/shard_map/all_to_all | solution.py:80
  60.3 2.4 collective-permute-start
  62.7 5.6 %collective-permute-start.1 = (bf16[128,2,1,128]{3,2,1,0:T(2,128)(2,1)S(1)}, bf16[128,2,1,128]{3,2,1,0:T(2,128)(2,1)S(1)}, u32[]{:S(2)}, u32[]{:S(2)}) collective-permute-start(bf16[128,2,1,128]{3,2,1,0:T(2,128)(2,1)S(1)} %get-tuple-element.40), channel_id=1, source_target_pairs={{2,0},{4,2},{6,4},{8,6},{10,8},{12,10},{14,12},{16,14},{18,16},{20... | collective-permute-start | bytes 196616 | tf_op jit(solution)/shard_map/ppermute | solution.py:18
  68.4 0.9 collective-permute-done
  69.2 1.6 collective-permute-done.1
  70.9 1.3 collective-permute-start.2
  72.2 1.3 collective-permute-start.3
  73.5 1.0 pad_maximum_fusion.4
  74.5 0.4 fusion.32
  75.3 2.0 maximum_maximum_fusion
  77.3 1.3 fusion.67
  81.2 0.4 convolution_add_fusion.10
  82.1 0.4 convolution_add_fusion.8
  82.6 0.8 copy-done.20
  83.3 1.1 fusion.5
  84.6 1.9 collective-permute-start.4
  86.5 6.6 %collective-permute-start.5 = (bf16[128,2,1,128]{3,2,1,0:T(2,128)(2,1)S(1)}, bf16[128,2,1,128]{3,2,1,0:T(2,128)(2,1)S(1)}, u32[]{:S(2)}, u32[]{:S(2)}) collective-permute-start(bf16[128,2,1,128]{3,2,1,0:T(2,128)(2,1)S(1)} %get-tuple-element.36), channel_id=1, source_target_pairs={{2,0},{4,2},{6,4},{8,6},{10,8},{12,10},{14,12},{16,14},{18,16},{20... | collective-permute-start | bytes 196616 | tf_op jit(solution)/shard_map/ppermute | solution.py:18
  93.2 0.5 convolution_bitcast_fusion.9
  93.7 1.6 collective-permute-done.4
  95.2 1.5 collective-permute-done.5
  96.8 1.3 collective-permute-start.6
  98.1 3.0 collective-permute-start.7
  101.1 1.0 pad_maximum_fusion.2
  102.2 0.4 fusion.30
  102.6 2.0 pad_maximum_fusion.1
  104.6 0.6 fusion.65
  105.2 0.6 fusion.66
  105.9 0.4 convolution_add_fusion.6
  106.3 0.4 convolution_add_fusion.5
  106.8 0.4 convolution_add_fusion.4
  107.2 0.4 convolution_add_fusion.3
  107.6 0.4 fusion.14
  108.1 0.4 convolution_add_fusion.2
  108.5 0.4 convolution_add_fusion.1
  109.0 1.4 fusion.3
  110.4 10.4 %all-to-all-start.1 = ((bf16[128,2,16,128]{3,2,1,0:T(8,128)(2,1)}), bf16[128,2,16,128]{3,2,1,0:T(8,128)(2,1)}, u32[]{:S(2)}, u32[]{:S(2)}) async-start(bf16[128,2,16,128]{3,2,1,0:T(8,128)(2,1)} %bitcast.251), calls=%async_computation.1 | async-start | bytes 2097152 | tf_op jit(solution)/shard_map/all_to_all | solution.py:112
  121.1 1.8 convolution_bitcast_fusion.10
  123.0 0.5 convolution_bitcast_fusion.8
  123.5 0.5 convolution_bitcast_fusion.5
  124.2 0.5 convolution_bitcast_fusion.7
  124.7 0.5 convolution_bitcast_fusion.6
  125.4 0.5 convolution_bitcast_fusion.3
  126.0 0.5 convolution_bitcast_fusion.2
  126.5 0.5 convolution_bitcast_fusion.4
  127.0 0.9 maximum_multiply_fusion
  127.8 23.3 %all-to-all-done.1 = bf16[128,2,16,128]{3,2,1,0:T(8,128)(2,1)} async-done(((bf16[128,2,16,128]{3,2,1,0:T(8,128)(2,1)}), bf16[128,2,16,128]{3,2,1,0:T(8,128)(2,1)}, u32[]{:S(2)}, u32[]{:S(2)}) %all-to-all-start.1) | async-done | bytes 1048608 | tf_op jit(solution)/shard_map/all_to_all | solution.py:112
  151.1 1.5 copy.12
  152.7 0.5 convolution_bitcast_fusion.11
  153.2 0.5 convolution_bitcast_fusion.12
  153.9 0.5 convolution_bitcast_fusion.13
  154.4 0.7 maximum_multiply_fusion.1
  155.4 107.3 %all-reduce.8.cloned.1.call-done = (f32[3,128,128]{2,1,0:T(8,128)}, f32[3,3,128,128]{3,2,1,0:T(8,128)}) async-done(((f32[3,128,128]{2,1,0:T(8,128)}, f32[3,3,128,128]{3,2,1,0:T(8,128)}), (f32[3,128,128]{2,1,0:T(8,128)}, f32[3,3,128,128]{3,2,1,0:T(8,128)})) %all-reduce.8.cloned.1.call-update) | async-done | bytes 786448 | tf_op jit(solution)/shard_map/psum | solution.py:139
  262.7 1.5 bitcast_multiply_fusion.2
  264.2 0.4 convolution_bitcast_fusion.1
  264.9 0.4 convolution_bitcast_fusion
  265.4 1.4 fusion.8
  266.9 73.0 %all-reduce.10.cloned.1.call-done = (f32[3,128,128]{2,1,0:T(8,128)}, f32[3,3,128,128]{3,2,1,0:T(8,128)}) async-done(((f32[3,128,128]{2,1,0:T(8,128)}, f32[3,3,128,128]{3,2,1,0:T(8,128)}), (f32[3,128,128]{2,1,0:T(8,128)}, f32[3,3,128,128]{3,2,1,0:T(8,128)})) %all-reduce.10.cloned.1.call-update) | async-done | bytes 786448 | tf_op jit(solution)/shard_map/psum | solution.py:138
  339.9 1.6 copy.20
  341.5 1.9 copy.21
  (73 shorter events, 7.6 us)
Async XLA Ops:
  7.2 3.1 copy-start.19
  10.2 1.8 copy-start.9
  10.2 1.6 copy-start.15
  12.0 1.0 copy-start.11
  12.0 1.3 copy-start.13
  60.3 9.0 %collective-permute-start = (bf16[128,2,1,128]{3,2,1,0:T(2,128)(2,1)S(1)}, bf16[128,2,1,128]{3,2,1,0:T(2,128)(2,1)S(1)}, u32[]{:S(2)}, u32[]{:S(2)}) collective-permute-start(bf16[128,2,1,128]{3,2,1,0:T(2,128)(2,1)S(1)} %get-tuple-element.39), channel_id=1, source_target_pairs={{0,2},{2,4},{4,6},{6,8},{8,10},{10,12},{12,14},{14,16},{16,18},{18... | collective-permute-start | bytes 196616 | tf_op jit(solution)/shard_map/ppermute | solution.py:16
  62.7 11.8 %copy-start.18 = (bf16[3,3,128,128]{3,2,1,0:T(8,128)(2,1)S(1)}, bf16[3,3,128,128]{3,2,1,0:T(8,128)(2,1)}, u32[]{:S(2)}) copy-start(bf16[3,3,128,128]{3,2,1,0:T(8,128)(2,1)} %param.9) | copy-start | bytes 884740
  62.7 8.1 %collective-permute-start.1 = (bf16[128,2,1,128]{3,2,1,0:T(2,128)(2,1)S(1)}, bf16[128,2,1,128]{3,2,1,0:T(2,128)(2,1)S(1)}, u32[]{:S(2)}, u32[]{:S(2)}) collective-permute-start(bf16[128,2,1,128]{3,2,1,0:T(2,128)(2,1)S(1)} %get-tuple-element.40), channel_id=1, source_target_pairs={{2,0},{4,2},{6,4},{8,6},{10,8},{12,10},{14,12},{16,14},{18,16},{20... | collective-permute-start | bytes 196616 | tf_op jit(solution)/shard_map/ppermute | solution.py:18
  70.9 4.1 %collective-permute-start.2 = (bf16[1,2,18,128]{3,2,1,0:T(8,128)(2,1)S(1)}, bf16[1,2,18,128]{3,2,1,0:T(8,128)(2,1)S(1)}, u32[]{:S(2)}, u32[]{:S(2)}) collective-permute-start(bf16[1,2,18,128]{3,2,1,0:T(8,128)(2,1)S(1)} %get-tuple-element.28), channel_id=1, source_target_pairs={{0,1},{2,3},{4,5},{6,7},{8,9},{10,11},{12,13},{14,15},{16,17},{18,... | collective-permute-start | bytes 27656 | tf_op jit(solution)/shard_map/ppermute | solution.py:16
  72.2 3.1 collective-permute-start.3
  74.5 8.0 %copy-start.16 = (bf16[128,2,16,128]{3,2,1,0:T(8,128)(2,1)}, bf16[128,2,16,128]{3,2,1,0:T(8,128)(2,1)S(1)}, u32[]{:S(2)}) copy-start(bf16[128,2,16,128]{3,2,1,0:T(8,128)(2,1)S(1)} %get-tuple-element.37) | copy-start | bytes 3145732
  78.6 1.0 copy-start
  78.6 1.4 copy-start.8
  78.6 1.8 copy-start.6
  78.6 2.2 copy-start.2
  78.6 3.0 copy-start.4
  82.1 1.2 copy-start.20
  84.6 10.6 %collective-permute-start.4 = (bf16[128,2,1,128]{3,2,1,0:T(2,128)(2,1)S(1)}, bf16[128,2,1,128]{3,2,1,0:T(2,128)(2,1)S(1)}, u32[]{:S(2)}, u32[]{:S(2)}) collective-permute-start(bf16[128,2,1,128]{3,2,1,0:T(2,128)(2,1)S(1)} %get-tuple-element.35), channel_id=1, source_target_pairs={{0,2},{2,4},{4,6},{6,8},{8,10},{10,12},{12,14},{14,16},{16,18},{18... | collective-permute-start | bytes 196616 | tf_op jit(solution)/shard_map/ppermute | solution.py:16
  86.5 10.2 %collective-permute-start.5 = (bf16[128,2,1,128]{3,2,1,0:T(2,128)(2,1)S(1)}, bf16[128,2,1,128]{3,2,1,0:T(2,128)(2,1)S(1)}, u32[]{:S(2)}, u32[]{:S(2)}) collective-permute-start(bf16[128,2,1,128]{3,2,1,0:T(2,128)(2,1)S(1)} %get-tuple-element.36), channel_id=1, source_target_pairs={{2,0},{4,2},{6,4},{8,6},{10,8},{12,10},{14,12},{16,14},{18,16},{20... | collective-permute-start | bytes 196616 | tf_op jit(solution)/shard_map/ppermute | solution.py:18
  96.8 5.8 %collective-permute-start.6 = (bf16[1,2,18,128]{3,2,1,0:T(8,128)(2,1)S(1)}, bf16[1,2,18,128]{3,2,1,0:T(8,128)(2,1)S(1)}, u32[]{:S(2)}, u32[]{:S(2)}) collective-permute-start(bf16[1,2,18,128]{3,2,1,0:T(8,128)(2,1)S(1)} %get-tuple-element.24), channel_id=1, source_target_pairs={{1,0},{3,2},{5,4},{7,6},{9,8},{11,10},{13,12},{15,14},{17,16},{19,... | collective-permute-start | bytes 27656 | tf_op jit(solution)/shard_map/ppermute | solution.py:18
  98.1 4.5 %collective-permute-start.7 = (bf16[1,2,18,128]{3,2,1,0:T(8,128)(2,1)S(1)}, bf16[1,2,18,128]{3,2,1,0:T(8,128)(2,1)S(1)}, u32[]{:S(2)}, u32[]{:S(2)}) collective-permute-start(bf16[1,2,18,128]{3,2,1,0:T(8,128)(2,1)S(1)} %get-tuple-element.25), channel_id=1, source_target_pairs={{0,1},{2,3},{4,5},{6,7},{8,9},{10,11},{12,13},{14,15},{16,17},{18,... | collective-permute-start | bytes 27656 | tf_op jit(solution)/shard_map/ppermute | solution.py:16
  110.4 40.7 %all-to-all-start.1 = ((bf16[128,2,16,128]{3,2,1,0:T(8,128)(2,1)}), bf16[128,2,16,128]{3,2,1,0:T(8,128)(2,1)}, u32[]{:S(2)}, u32[]{:S(2)}) async-start(bf16[128,2,16,128]{3,2,1,0:T(8,128)(2,1)} %bitcast.251), calls=%async_computation.1 | async-start | bytes 2097152 | tf_op jit(solution)/shard_map/all_to_all | solution.py:112
  120.8 141.9 %all-reduce.8.cloned.1.call-start = ((), (), s32[]{:S(2)}) async-start(), calls=%async_computation.2 | async-start | bytes 1572864 | tf_op jit(solution)/shard_map/psum | solution.py:139
  121.1 1.9 copy-start.7
  121.1 2.4 copy-start.5
  123.0 1.2 copy-start.3
  124.2 1.2 copy-start.17
  124.7 1.3 copy-start.1
  126.9 25.7 %copy-start.14 = (bf16[1,16,256,128]{3,2,1,0:T(8,128)(2,1)S(1)}, bf16[1,16,256,128]{3,2,1,0:T(8,128)(2,1)}, u32[]{:S(2)}) copy-start(bf16[1,16,256,128]{3,2,1,0:T(8,128)(2,1)} %copy-done.13) | copy-start | bytes 3145732
  151.1 2.0 copy-start.12
  152.7 1.2 copy-start.10
  155.1 184.8 %all-reduce.10.cloned.1.call-start = ((), (), s32[]{:S(2)}) async-start(), calls=%async_computation.3 | async-start | bytes 1572864 | tf_op jit(solution)/shard_map/psum | solution.py:138
Sparse Core Ops, SparseCore 0:
  155.2 107.4 all-reduce.7
  265.1 74.6 all-reduce.9
